TPU v7x, 32 devices: a whole 2x2x4 slice. The times are simulated.
32 devices in a mesh: dom: 16 (over z, x, core), feat: 2 (over y).
Axes of the slice: x: 2, y: 2, z: 4, core: 2. Of those that a mesh axis runs over, the one named last changes fastest.
Arguments:
- features: bfloat16 [65536, 1024], P('dom', 'feat'), may hold values from -6 to 6
- w_self: bfloat16 [1024, 256], P('feat'), may hold values from -0.1875 to 0.1875
- w_neigh: bfloat16 [1024, 256], P('feat'), may hold values from -0.1875 to 0.1875
- hidden_bias: float32 [256], replicated, may hold values from -3 to 3
- edge_tiles: bfloat16 [16, 102, 128, 128], P('dom'), may hold values from 0 to 0.099609375
- tile_dst: int32 [16, 102], P('dom'), may hold values from 0 to 31, as said below
- tile_src: int32 [16, 102], P('dom'), may hold values from 0 to 47, as said below
- tile_count: int32 [16], P('dom'), may hold values from 12 to 102, as said below
- bound_rows: int32 [16, 256], P('dom'), may hold values from 0 to 4095, as said below
- send_pick: int32 [16, 16, 128], P('dom'), may hold values from 0 to 255, as said below
- cotangent: bfloat16 [65536, 256], P(('dom', 'feat')), may hold values from -0.0234375 to 0.0234375
Outputs:
- hidden: bfloat16 [65536, 256], P(('dom', 'feat'))
- grad_self: bfloat16 [1024, 256], P('feat')
- grad_neigh: bfloat16 [1024, 256], P('feat')
- grad_bias: float32 [256], replicated
Inputs may be any that keep to these rules, and one draw needn't show every extreme that they name: Within a partition the pairs (tile_dst, tile_src) of its 102 slots are distinct. `tile_src`: A source block below 32 is a row tile of the partition itself; block 32 + q is the block received from partition q. Slots from tile_count[p] on are unused. Some partition uses all 102 slots. `bound_rows`: distinct within each partition. Each list send_pick[p, q] has no repeats.
All inputs are finite; a program needn't handle non-finite values.
Results may differ from a plain program's by a relative error of at most 0.009.
The roundings to bfloat16 on the way count: a program that leaves them out, or rounds other values in their place, can miss the bound.
Values may be sent and summed in bfloat16 or wider, within the bound.
A program may use at most 128 MiB of HBM per device.

v0:
```python
import jax
import jax.numpy as jnp
from jax import lax
from jax.sharding import PartitionSpec as P

TILE = 128


def tile_sums(source, local_tiles, dest_list, source_list, live_count, dest_tiles):
    slice_width = source.shape[1]
    blocks = source.reshape(source.shape[0] // TILE, TILE, slice_width)
    picked = jnp.take(blocks, source_list, axis=0)
    products = jnp.einsum("etc,ecf->etf", local_tiles, picked, preferred_element_type=jnp.float32)
    slot_ids = jnp.arange(source_list.shape[0], dtype=jnp.int32)
    live_slots = (slot_ids < live_count).astype(jnp.float32)
    dest_ids = jnp.arange(dest_tiles, dtype=jnp.int32)[:, None]
    onehot = (dest_list[None, :] == dest_ids).astype(jnp.float32) * live_slots[None, :]
    summed = jnp.einsum("de,etf->dtf", onehot, products, precision=lax.Precision.HIGHEST)
    return summed.reshape(dest_tiles * TILE, slice_width).astype(jnp.bfloat16)


def body(
    features,
    w_self,
    w_neigh,
    hidden_bias,
    edge_tiles,
    tile_dst,
    tile_src,
    tile_count,
    bound_rows,
    send_pick,
    cotangent,
):
    part_count = lax.axis_size("dom")
    slice_width = features.shape[1]
    node_rows = features.shape[0]
    boundary = jnp.take(features, bound_rows[0], axis=0)
    everyone = lax.all_gather(boundary, "dom", axis=0, tiled=True)
    pick_lists = lax.all_to_all(send_pick, "dom", split_axis=1, concat_axis=0, tiled=True)
    offsets = (jnp.arange(part_count, dtype=jnp.int32) * boundary.shape[0])[:, None]
    wanted = (pick_lists[:, 0, :] + offsets).reshape(-1)
    received = jnp.take(everyone, wanted, axis=0)
    source = jnp.concatenate([features, received], 0)
    aggregated = tile_sums(
        source, edge_tiles[0], tile_dst[0], tile_src[0], tile_count[0], node_rows // TILE
    )
    stacked = jnp.concatenate([features, aggregated], 1)
    weights = jnp.concatenate([w_self, w_neigh], 0)
    row_block = stacked
    summed = lax.psum_scatter(
        jnp.dot(row_block, weights, preferred_element_type=jnp.float32),
        "feat",
        scatter_dimension=0,
        tiled=True,
    )
    preact = summed + hidden_bias
    hidden = jnp.maximum(preact, 0.0).astype(jnp.bfloat16)
    pre_grad = jnp.where(preact > 0.0, cotangent, jnp.zeros_like(cotangent))
    shard_rows = lax.all_gather(pre_grad, "feat", axis=0, tiled=True)
    row_block = stacked
    product = lax.dot_general(
        row_block, shard_rows, (((0,), (0,)), ((), ())), preferred_element_type=jnp.float32
    )
    all_grads = product
    bias_grad = jnp.sum(shard_rows.astype(jnp.float32), 0)
    all_grads, bias_grad = lax.psum((all_grads, bias_grad), "dom")
    grad_self = all_grads[:slice_width]
    grad_neigh = all_grads[slice_width:]
    return (hidden, grad_self.astype(jnp.bfloat16), grad_neigh.astype(jnp.bfloat16), bias_grad)


def solution(mesh):
    placed = (
        P("dom", "feat"),
        P("feat", None),
        P("feat", None),
        P(),
        P("dom", None, None, None),
        P("dom", None),
        P("dom", None),
        P("dom"),
        P("dom", None),
        P("dom", None, None),
        P(("dom", "feat"), None),
    )
    return jax.shard_map(
        body,
        mesh=mesh,
        in_specs=placed,
        out_specs=(P(("dom", "feat"), None), P("feat", None), P("feat", None), P()),
        check_vma=False,
    )
```

profile of v0, /device:TPU:0, one launch (start us, length us, event | category | flops | bytes accessed | tf_op | source)
XLA Modules:
  0.0 343.9 jit_solution(6246623295148714957)
XLA Ops:
  7.2 0.8 compare_select_fusion.3
  8.9 4.6 %gather_fusion = bf16[256,512]{1,0:T(8,128)(2,1)} fusion(bf16[4096,512]{1,0:T(8,128)(2,1)} %param.11, s32[1024]{0:T(1024)S(1)} %pad_clamp_fusion.1), kind=kCustom, calls=%fused_computation | custom fusion | bytes 525312 | tf_op jit(solution)/shard_map/jit(_take)/gather | solution.py:38
  13.5 1.8 broadcast_select_fusion.1
  15.3 7.4 %all-to-all-start = ((s32[1,16,128]{2,0,1:T(1,128)}), s32[1,16,128]{2,0,1:T(1,128)S(1)}, u32[]{:S(2)}, u32[]{:S(2)}) async-start(s32[1,16,128]{2,0,1:T(1,128)} %bitcast.45), calls=%async_computation | async-start | bytes 16384 | tf_op jit(solution)/shard_map/all_to_all | solution.py:40
  24.7 4.3 %all-to-all-done = s32[1,16,128]{2,0,1:T(1,128)S(1)} async-done(((s32[1,16,128]{2,0,1:T(1,128)}), s32[1,16,128]{2,0,1:T(1,128)S(1)}, u32[]{:S(2)}, u32[]{:S(2)}) %all-to-all-start) | async-done | bytes 8224 | tf_op jit(solution)/shard_map/all_to_all | solution.py:40
  29.2 39.3 %all-gather.3.cloned.1.call-done = bf16[4096,512]{1,0:T(8,128)(2,1)} async-done(((bf16[256,512]{1,0:T(8,128)(2,1)}), bf16[4096,512]{1,0:T(8,128)(2,1)}) %all-gather.3.cloned.1.call-update) | async-done | bytes 4194320 | tf_op jit(solution)/shard_map/all_gather | solution.py:39
  68.5 12.2 %gather_fusion.1 = bf16[2048,512]{1,0:T(8,128)(2,1)} fusion(bf16[4096,512]{1,0:T(8,128)(2,1)} %all-gather.3.cloned.1.call-done, s32[2048]{0:T(1024)S(1)} %broadcast_clamp_fusion), kind=kCustom, calls=%fused_computation.1 | custom fusion | bytes 4202496 | tf_op jit(solution)/shard_map/jit(_take)/gather | solution.py:43
  80.7 1.9 broadcast_select_fusion
  82.6 0.9 copy-done.2
  83.5 3.0 pad_maximum_fusion.1
  86.5 10.2 %gather_fusion.2 = bf16[102,128,512]{2,1,0:T(8,128)(2,1)} fusion(bf16[48,128,512]{2,1,0:T(8,128)(2,1)} %bitcast.39, s32[1024]{0:T(1024)S(1)} %pad_clamp_fusion), kind=kCustom, calls=%fused_computation.2 | custom fusion | bytes 26739096 | tf_op jit(solution)/shard_map/jit(_take)/gather | solution.py:12
  96.7 13.8 %fusion.3 = f32[102,128,512]{1,2,0:T(8,128)} fusion(bf16[102,128,512]{2,1,0:T(8,128)(2,1)} %gather_fusion.2, pred[102]{0:T(512)(128)(4,1)S(1)} %compare_and_fusion.2, bf16[1,102,128,128]{3,2,1,0:T(8,128)(2,1)S(1)} %copy-done), kind=kOutput, calls=%fused_computation.6 | convolution fusion | flops 1717960704 | bytes 43450472 | tf_op jit(solution)/shard_map/etc,ecf->etf/dot_general | solution.py:13
  110.5 28.4 %copy.21 = f32[102,128,512]{2,0,1:T(8,128)} copy(f32[102,128,512]{1,2,0:T(8,128)} %fusion.3) | data formatting | bytes 53477376 | tf_op jit(solution)/shard_map/etc,ecf->etf/dot_general | solution.py:13
  139.0 16.6 %convolution_convert_fusion = bf16[32,128,512]{2,0,1:T(8,128)(2,1)S(1)} fusion(f32[102,128,512]{2,0,1:T(8,128)} %copy.21, f32[102]{0:T(128)S(1)} %compare_convert_fusion, s32[102]{0:T(128)S(1)} %bitcast.48), kind=kOutput, calls=%fused_computation.14 | convolution fusion | flops 2569017856 | bytes 30933808 | tf_op jit(solution)/shard_map/de,etf->dtf/dot_general | solution.py:18
  155.6 2.4 copy.22
  158.0 2.0 copy-done.5
  159.9 3.9 %fusion.8 = f32[4096,256]{1,0:T(8,128)} fusion(bf16[4096,512]{1,0:T(8,128)(2,1)S(1)} %bitcast.40, bf16[4096,512]{1,0:T(8,128)(2,1)S(1)} %copy-done.3, bf16[512,256]{1,0:T(8,128)(2,1)S(1)} %copy-done.10, bf16[512,256]{1,0:T(8,128)(2,1)S(1)} %copy-done.11), kind=kOutput, calls=%fused_computation.11 | convolution fusion | flops 2165309440 | bytes 13107200 | tf_op jit(solution)/shard_map/dot_general | solution.py:52
  164.1 52.8 %reduce-scatter.2.cloned.1.call-done = f32[2048,256]{1,0:T(8,128)} async-done(((f32[4096,256]{1,0:T(8,128)}), f32[2048,256]{1,0:T(8,128)}) %reduce-scatter.2.cloned.1.call-update) | async-done | bytes 2097168 | tf_op jit(solution)/shard_map/reduce_scatter | solution.py:51
  216.9 3.0 compare_select_fusion
  220.0 1.2 maximum_convert_fusion
  221.2 32.1 %all-gather.5.cloned.1.call-done = bf16[4096,256]{1,0:T(8,128)(2,1)} async-done(((bf16[2048,256]{1,0:T(8,128)(2,1)}), bf16[4096,256]{1,0:T(8,128)(2,1)}) %all-gather.5.cloned.1.call-update) | async-done | bytes 2097168 | tf_op jit(solution)/shard_map/all_gather | solution.py:60
  253.3 7.6 %fusion.7 = f32[1024,256]{1,0:T(8,128)} fusion(bf16[4096,256]{1,0:T(8,128)(2,1)} %all-gather.5.cloned.1.call-done, bf16[4096,512]{1,0:T(8,128)(2,1)} %bitcast.41, bf16[4096,512]{1,0:T(8,128)(2,1)} %param.11), kind=kOutput, calls=%fused_computation.10 | convolution fusion | flops 2164260864 | bytes 11534336 | tf_op jit(solution)/shard_map/dot_general | solution.py:62
  261.4 74.1 %all-reduce.2 = (bf16[1024,256]{1,0:T(8,128)(2,1)}, f32[256]{0:T(256)}) all-reduce(f32[1024,256]{1,0:T(8,128)} %fusion.7, f32[256]{0:T(256)S(1)} %convert_reduce_fusion), channel_id=1, replica_groups=mesh['dom'=16,'feat'=2] {'dom'}, use_global_device_ids=true, to_apply=%region_1.2 | all-reduce | flops 262400 | bytes 1574912 | tf_op jit(solution)/shard_map/psum | solution.py:67
  335.5 1.9 fusion.23
  (40 shorter events, 3.3 us)
Async XLA Ops:
  7.2 89.6 %copy-start = (bf16[1,102,128,128]{3,2,1,0:T(8,128)(2,1)S(1)}, bf16[1,102,128,128]{3,2,1,0:T(8,128)(2,1)}, u32[]{:S(2)}) copy-start(bf16[1,102,128,128]{3,2,1,0:T(8,128)(2,1)} %param.15) | copy-start | bytes 10027012
  7.2 61.4 %all-gather.3.cloned.1.call-start = ((), (), s32[]{:S(2)}) async-start(), calls=%async_computation.2 | async-start | bytes 4456448 | tf_op jit(solution)/shard_map/all_gather | solution.py:39
  15.3 13.8 %all-to-all-start = ((s32[1,16,128]{2,0,1:T(1,128)}), s32[1,16,128]{2,0,1:T(1,128)S(1)}, u32[]{:S(2)}, u32[]{:S(2)}) async-start(s32[1,16,128]{2,0,1:T(1,128)} %bitcast.45), calls=%async_computation | async-start | bytes 16384 | tf_op jit(solution)/shard_map/all_to_all | solution.py:40
  22.7 194.2 %reduce-scatter.2.cloned.1.call-start = ((), (), s32[]{:S(2)}) async-start(), calls=%async_computation.3 | async-start | bytes 6291456 | tf_op jit(solution)/shard_map/reduce_scatter | solution.py:51
  80.7 2.8 copy-start.2
  110.5 28.4 %copy-start.9 = (s32[1,102]{1,0:T(1,128)S(1)}, s32[1,102]{1,0:T(1,128)}, u32[]{:S(2)}) copy-start(s32[1,102]{1,0:T(1,128)} %param.16) | copy-start | bytes 1228
  155.5 4.4 %copy-start.3 = (bf16[4096,512]{1,0:T(8,128)(2,1)S(1)}, bf16[4096,512]{1,0:T(8,128)(2,1)}, u32[]{:S(2)}) copy-start(bf16[4096,512]{1,0:T(8,128)(2,1)} %param.11) | copy-start | bytes 12582916
  155.5 4.4 %copy-start.10 = (bf16[512,256]{1,0:T(8,128)(2,1)S(1)}, bf16[512,256]{1,0:T(8,128)(2,1)}, u32[]{:S(2)}) copy-start(bf16[512,256]{1,0:T(8,128)(2,1)} %param.13) | copy-start | bytes 786436
  155.6 4.4 %copy-start.11 = (bf16[512,256]{1,0:T(8,128)(2,1)S(1)}, bf16[512,256]{1,0:T(8,128)(2,1)}, u32[]{:S(2)}) copy-start(bf16[512,256]{1,0:T(8,128)(2,1)} %param.12) | copy-start | bytes 786436
  158.0 2.0 copy-start.5
  163.8 53.1 %copy-start.7 = (bf16[2048,256]{1,0:T(8,128)(2,1)S(1)}, bf16[2048,256]{1,0:T(8,128)(2,1)}, u32[]{:S(2)}) copy-start(bf16[2048,256]{1,0:T(8,128)(2,1)} %param.21) | copy-start | bytes 3145732
  163.8 53.1 %copy-start.8 = (f32[256]{0:T(256)S(1)}, f32[256]{0:T(256)}, u32[]{:S(2)}) copy-start(f32[256]{0:T(256)} %param.14) | copy-start | bytes 3076
  163.8 89.4 %all-gather.5.cloned.1.call-start = ((), (), s32[]{:S(2)}) async-start(), calls=%async_computation.4 | async-start | bytes 3145728 | tf_op jit(solution)/shard_map/all_gather | solution.py:60
  216.9 3.1 copy-start.4
  253.3 7.6 %copy-start.6 = (bf16[4096,256]{1,0:T(8,128)(2,1)S(1)}, bf16[4096,256]{1,0:T(8,128)(2,1)}, u32[]{:S(2)}) copy-start(bf16[4096,256]{1,0:T(8,128)(2,1)} %all-gather.5.cloned.1.call-done) | copy-start | bytes 6291460
  253.3 84.1 %copy-start.1 = (bf16[1,102,128,128]{3,2,1,0:T(8,128)(2,1)S(1)}, bf16[1,102,128,128]{3,2,1,0:T(8,128)(2,1)}, u32[]{:S(2)}) copy-start(bf16[1,102,128,128]{3,2,1,0:T(8,128)(2,1)} %param.15) | copy-start | bytes 10027012
Sparse Core Ops, SparseCore 0:
  15.4 53.0 all-gather.2
  164.0 52.9 reduce-scatter.1
  220.1 33.1 all-gather.4
where the time goes:
time: 345 us; the launch traced here: 344 us
  waiting for transfers between devices  129 us (37%)
  blocking collectives  74.1 us (21%)
  local copies, waits for them, and re-layouts  62.7 us (18%)
  matrix products  41.8 us (12%)
  other arithmetic  14.5 us (4%)
  between operations  14.5 us (4%)
  starting transfers between devices  7.74 us (2%)
    psum x1, blocking collectives, body(): all_grads, bias_grad = lax.psum((all_grads, bias_grad), 'dom')  74.1 us
    reduce_scatter x1, waiting for transfers between devices, body(): lax.psum_scatter(jnp.dot(row_block, weights, preferred_element_type=jnp.f...  52.8 us
    all_gather x1, waiting for transfers between devices, body(): everyone = lax.all_gather(boundary, 'dom', axis=0, tiled=True)  39.3 us
    all_gather x1, waiting for transfers between devices, body(): shard_rows = lax.all_gather(pre_grad, 'feat', axis=0, tiled=True)  32.1 us
    dot_general x1, local copies, waits for them, and re-layouts, tile_sums(): jnp.einsum('etc,ecf->etf', local_tiles, picked, preferred_element_type=jn...  28.4 us
    dot_general x1, matrix products, tile_sums(): jnp.einsum('de,etf->dtf', onehot, products, precision=lax.Precision.HIGHEST)  16.6 us
    dot_general x1, matrix products, tile_sums(): jnp.einsum('etc,ecf->etf', local_tiles, picked, preferred_element_type=jn...  13.8 us
    gather x1, local copies, waits for them, and re-layouts, body(): received = jnp.take(everyone, wanted, axis=0)  12.2 us
  transfers between devices with their start and end apart: 4, of which 4 were waited for; matrix products, arithmetic and copies ran while one was open for 1% of the time, Pallas kernels for 0%

commit v1 on v0

--- a/solution.py
+++ b/solution.py
@@ -4,6 +4,24 @@
 from jax.sharding import PartitionSpec as P
 
 TILE = 128
+
+
+def gather_around(shard, axis, dim):
+    ways, here, lap = (lax.axis_size(axis), lax.axis_index(axis), shard.shape[dim])
+    shape = [n * ways if d == dim else n for d, n in enumerate(shard.shape)]
+    full = lax.dynamic_update_slice_in_dim(
+        jnp.zeros(shape, shard.dtype), shard, here * lap, axis=dim
+    )
+    going_up = going_down = shard
+    for far in range(1, ways // 2 + 1):
+        going_up = lax.ppermute(going_up, axis, [(d, (d + 1) % ways) for d in range(ways)])
+        full = lax.dynamic_update_slice_in_dim(full, going_up, (here - far) % ways * lap, axis=dim)
+        if 2 * far < ways:
+            going_down = lax.ppermute(going_down, axis, [(d, (d - 1) % ways) for d in range(ways)])
+            full = lax.dynamic_update_slice_in_dim(
+                full, going_down, (here + far) % ways * lap, axis=dim
+            )
+    return full
 
 
 def tile_sums(source, local_tiles, dest_list, source_list, live_count, dest_tiles):
@@ -36,7 +54,7 @@
     slice_width = features.shape[1]
     node_rows = features.shape[0]
     boundary = jnp.take(features, bound_rows[0], axis=0)
-    everyone = lax.all_gather(boundary, "dom", axis=0, tiled=True)
+    everyone = gather_around(boundary, "dom", 0)
     pick_lists = lax.all_to_all(send_pick, "dom", split_axis=1, concat_axis=0, tiled=True)
     offsets = (jnp.arange(part_count, dtype=jnp.int32) * boundary.shape[0])[:, None]
     wanted = (pick_lists[:, 0, :] + offsets).reshape(-1)

time: 345 us -> 365 us (1.058)
  starting transfers between devices: 7.74 us -> 36.9 us
  waiting for transfers between devices: 129 us -> 103 us
  local copies, waits for them, and re-layouts: 62.7 us -> 80.5 us
    all_gather x1 -> x0, waiting for transfers between devices: 39.3 us -> none  [body(): everyone = lax.all_gather(boundary, 'dom', axis=0, tiled=True)]
    ppermute x0 -> x15, starting transfers between devices: none -> 32.9 us  [the longest x7 32.4 us: gather_around(): lax.ppermute(going_down, axis, [(d, (d - 1) % ways) for d in range(ways)])]
    ppermute x0 -> x15, waiting for transfers between devices: none -> 18.9 us  [the longest x8 16 us: gather_around(): lax.ppermute(going_up, axis, [(d, (d + 1) % ways) for d in range(ways)])]
    dynamic_update_slice x0 -> x15, local copies, waits for them, and re-layouts: none -> 15.6 us  [the longest x8 8.63 us: gather_around(): lax.dynamic_update_slice_in_dim(full, going_up, (here - far) % ways * lap...]
    all_to_all x1, waiting for transfers between devices: 4.32 us -> 0.01 us  [body(): lax.all_to_all(send_pick, 'dom', split_axis=1, concat_axis=0, tiled=True)]
    all_to_all x1, starting transfers between devices: 7.4 us -> 3.67 us  [body(): lax.all_to_all(send_pick, 'dom', split_axis=1, concat_axis=0, tiled=True)]
  transfers between devices with their start and end apart: 4 -> 18, of which waited for: 4 -> 13; matrix products, arithmetic and copies ran while one was open for 1% -> 4% of each run, Pallas kernels for 0% -> 0%
where the time goes in v1:
time: 365 us; the launch traced here: 364 us
  waiting for transfers between devices  103 us (28%)
  local copies, waits for them, and re-layouts  80.5 us (22%)
  blocking collectives  74.1 us (20%)
  matrix products  41.8 us (11%)
  starting transfers between devices  36.9 us (10%)
  between operations  15.2 us (4%)
  other arithmetic  12.4 us (3%)
    psum x1, blocking collectives, body(): all_grads, bias_grad = lax.psum((all_grads, bias_grad), 'dom')  74.1 us
    reduce_scatter x1, waiting for transfers between devices, body(): lax.psum_scatter(jnp.dot(row_block, weights, preferred_element_type=jnp.f...  52 us
    ppermute x7, starting transfers between devices, gather_around(): lax.ppermute(going_down, axis, [(d, (d - 1) % ways) for d in range(ways)])  32.4 us
    all_gather x1, waiting for transfers between devices, body(): shard_rows = lax.all_gather(pre_grad, 'feat', axis=0, tiled=True)  32.1 us
    dot_general x1, local copies, waits for them, and re-layouts, tile_sums(): jnp.einsum('etc,ecf->etf', local_tiles, picked, preferred_element_type=jn...  28.4 us
    dot_general x1, matrix products, tile_sums(): jnp.einsum('de,etf->dtf', onehot, products, precision=lax.Precision.HIGHEST)  16.6 us
    ppermute x8, waiting for transfers between devices, gather_around(): lax.ppermute(going_up, axis, [(d, (d + 1) % ways) for d in range(ways)])  16 us
    dot_general x1, matrix products, tile_sums(): jnp.einsum('etc,ecf->etf', local_tiles, picked, preferred_element_type=jn...  13.8 us
  transfers between devices with their start and end apart: 18, of which 13 were waited for; matrix products, arithmetic and copies ran while one was open for 4% of the time, Pallas kernels for 0%

profile of v1, /device:TPU:0, one launch (start us, length us, event | category | flops | bytes accessed | tf_op | source)
XLA Modules:
  0.0 363.9 jit_solution(17713927793604850750)
XLA Ops:
  8.9 4.6 %gather_fusion = bf16[256,512]{1,0:T(8,128)(2,1)} fusion(bf16[4096,512]{1,0:T(8,128)(2,1)} %param.11, s32[1024]{0:T(1024)S(1)} %pad_clamp_fusion.1), kind=kCustom, calls=%fused_computation | custom fusion | bytes 525312 | tf_op jit(solution)/shard_map/jit(_take)/gather | solution.py:56
  17.2 4.9 %collective-permute-start.1 = (bf16[256,512]{1,0:T(8,128)(2,1)}, bf16[256,512]{1,0:T(8,128)(2,1)}, u32[]{:S(2)}, u32[]{:S(2)}) collective-permute-start(bf16[256,512]{1,0:T(8,128)(2,1)} %get-tuple-element.7), channel_id=1, source_target_pairs={{0,30},{2,0},{4,2},{6,4},{8,6},{10,8},{12,10},{14,12},{16,14},{18,... | collective-permute-start | bytes 786440 | tf_op jit(solution)/shard_map/ppermute | solution.py:20
  22.1 3.7 %all-to-all-start = ((s32[1,16,128]{2,0,1:T(1,128)}), s32[1,16,128]{2,0,1:T(1,128)S(1)}, u32[]{:S(2)}, u32[]{:S(2)}) async-start(s32[1,16,128]{2,0,1:T(1,128)} %bitcast.4), calls=%async_computation | async-start | bytes 16384 | tf_op jit(solution)/shard_map/all_to_all | solution.py:58
  27.6 4.5 %collective-permute-start.3 = (bf16[256,512]{1,0:T(8,128)(2,1)}, bf16[256,512]{1,0:T(8,128)(2,1)}, u32[]{:S(2)}, u32[]{:S(2)}) collective-permute-start(bf16[256,512]{1,0:T(8,128)(2,1)} %collective-permute-done.1), channel_id=1, source_target_pairs={{0,30},{2,0},{4,2},{6,4},{8,6},{10,8},{12,10},{14,12},{16,14},{18,... | collective-permute-start | bytes 786440 | tf_op jit(solution)/shard_map/ppermute | solution.py:20
  32.1 3.5 collective-permute-done.2
  36.3 4.7 %collective-permute-start.5 = (bf16[256,512]{1,0:T(8,128)(2,1)}, bf16[256,512]{1,0:T(8,128)(2,1)S(1)}, u32[]{:S(2)}, u32[]{:S(2)}) collective-permute-start(bf16[256,512]{1,0:T(8,128)(2,1)} %collective-permute-done.3), channel_id=1, source_target_pairs={{0,30},{2,0},{4,2},{6,4},{8,6},{10,8},{12,10},{14,12},{16,14},{18,... | collective-permute-start | bytes 786440 | tf_op jit(solution)/shard_map/ppermute | solution.py:20
  41.0 3.5 collective-permute-done.4
  46.2 4.4 %collective-permute-start.7 = (bf16[256,512]{1,0:T(8,128)(2,1)S(1)}, bf16[256,512]{1,0:T(8,128)(2,1)S(1)}, u32[]{:S(2)}, u32[]{:S(2)}) collective-permute-start(bf16[256,512]{1,0:T(8,128)(2,1)S(1)} %collective-permute-done.5), channel_id=1, source_target_pairs={{0,30},{2,0},{4,2},{6,4},{8,6},{10,8},{12,10},{14,12},{16,14},{18,... | collective-permute-start | bytes 786440 | tf_op jit(solution)/shard_map/ppermute | solution.py:20
  56.6 4.5 %collective-permute-start.9 = (bf16[256,512]{1,0:T(8,128)(2,1)S(1)}, bf16[256,512]{1,0:T(8,128)(2,1)S(1)}, u32[]{:S(2)}, u32[]{:S(2)}) collective-permute-start(bf16[256,512]{1,0:T(8,128)(2,1)S(1)} %collective-permute-done.7), channel_id=1, source_target_pairs={{0,30},{2,0},{4,2},{6,4},{8,6},{10,8},{12,10},{14,12},{16,14},{18,... | collective-permute-start | bytes 786440 | tf_op jit(solution)/shard_map/ppermute | solution.py:20
  64.9 4.7 %collective-permute-start.11 = (bf16[256,512]{1,0:T(8,128)(2,1)S(1)}, bf16[256,512]{1,0:T(8,128)(2,1)S(1)}, u32[]{:S(2)}, u32[]{:S(2)}) collective-permute-start(bf16[256,512]{1,0:T(8,128)(2,1)S(1)} %collective-permute-done.9), channel_id=1, source_target_pairs={{0,30},{2,0},{4,2},{6,4},{8,6},{10,8},{12,10},{14,12},{16,14},{18,... | collective-permute-start | bytes 786440 | tf_op jit(solution)/shard_map/ppermute | solution.py:20
  73.5 4.7 %collective-permute-start.13 = (bf16[256,512]{1,0:T(8,128)(2,1)S(1)}, bf16[256,512]{1,0:T(8,128)(2,1)S(1)}, u32[]{:S(2)}, u32[]{:S(2)}) collective-permute-start(bf16[256,512]{1,0:T(8,128)(2,1)S(1)} %collective-permute-done.11), channel_id=1, source_target_pairs={{0,30},{2,0},{4,2},{6,4},{8,6},{10,8},{12,10},{14,12},{16,14},{18,... | collective-permute-start | bytes 786440 | tf_op jit(solution)/shard_map/ppermute | solution.py:20
  82.8 5.6 %collective-permute-done.14 = bf16[256,512]{1,0:T(8,128)(2,1)S(1)} collective-permute-done((bf16[256,512]{1,0:T(8,128)(2,1)S(1)}, bf16[256,512]{1,0:T(8,128)(2,1)S(1)}, u32[]{:S(2)}, u32[]{:S(2)}) %collective-permute-start.14) | collective-permute-done | bytes 262176 | tf_op jit(solution)/shard_map/ppermute | solution.py:17
  89.1 12.2 %gather_fusion.1 = bf16[2048,512]{1,0:T(8,128)(2,1)} fusion(bf16[4096,512]{1,0:T(8,128)(2,1)} %constant_dynamic-update-slice_fusion, s32[2048]{0:T(1024)S(1)} %broadcast_clamp_fusion), kind=kCustom, calls=%fused_computation.1 | custom fusion | bytes 4202496 | tf_op jit(solution)/shard_map/jit(_take)/gather | solution.py:61
  104.1 3.0 pad_maximum_fusion.1
  107.1 10.2 %gather_fusion.2 = bf16[102,128,512]{2,1,0:T(8,128)(2,1)} fusion(bf16[48,128,512]{2,1,0:T(8,128)(2,1)} %bitcast.39, s32[1024]{0:T(1024)S(1)} %pad_clamp_fusion), kind=kCustom, calls=%fused_computation.2 | custom fusion | bytes 26739096 | tf_op jit(solution)/shard_map/jit(_take)/gather | solution.py:30
  117.3 13.8 %fusion.3 = f32[102,128,512]{1,2,0:T(8,128)} fusion(bf16[102,128,512]{2,1,0:T(8,128)(2,1)} %gather_fusion.2, pred[102]{0:T(512)(128)(4,1)S(1)} %compare_and_fusion.2, bf16[1,102,128,128]{3,2,1,0:T(8,128)(2,1)S(1)} %copy-done), kind=kOutput, calls=%fused_computation.6 | convolution fusion | flops 1717960704 | bytes 43450472 | tf_op jit(solution)/shard_map/etc,ecf->etf/dot_general | solution.py:31
  131.1 28.4 %copy.21 = f32[102,128,512]{2,0,1:T(8,128)} copy(f32[102,128,512]{1,2,0:T(8,128)} %fusion.3) | data formatting | bytes 53477376 | tf_op jit(solution)/shard_map/etc,ecf->etf/dot_general | solution.py:31
  159.5 16.6 %convolution_convert_fusion = bf16[32,128,512]{2,0,1:T(8,128)(2,1)S(1)} fusion(f32[102,128,512]{2,0,1:T(8,128)} %copy.21, f32[102]{0:T(128)S(1)} %compare_convert_fusion, s32[102]{0:T(128)S(1)} %bitcast.47), kind=kOutput, calls=%fused_computation.14 | convolution fusion | flops 2569017856 | bytes 30933808 | tf_op jit(solution)/shard_map/de,etf->dtf/dot_general | solution.py:36
  180.5 3.9 %fusion.8 = f32[4096,256]{1,0:T(8,128)} fusion(bf16[4096,512]{1,0:T(8,128)(2,1)S(1)} %bitcast.40, bf16[4096,512]{1,0:T(8,128)(2,1)S(1)} %copy-done.3, bf16[512,256]{1,0:T(8,128)(2,1)S(1)} %copy-done.11, bf16[512,256]{1,0:T(8,128)(2,1)S(1)} %copy-done.12), kind=kOutput, calls=%fused_computation.11 | convolution fusion | flops 2165309440 | bytes 13107200 | tf_op jit(solution)/shard_map/dot_general | solution.py:70
  184.7 52.0 %reduce-scatter.2.cloned.1.call-done = f32[2048,256]{1,0:T(8,128)} async-done(((f32[4096,256]{1,0:T(8,128)}), f32[2048,256]{1,0:T(8,128)}) %reduce-scatter.2.cloned.1.call-update) | async-done | bytes 2097168 | tf_op jit(solution)/shard_map/reduce_scatter | solution.py:69
  236.7 3.0 compare_select_fusion
  240.9 32.1 %all-gather.2.cloned.1.call-done = bf16[4096,256]{1,0:T(8,128)(2,1)} async-done(((bf16[2048,256]{1,0:T(8,128)(2,1)}), bf16[4096,256]{1,0:T(8,128)(2,1)}) %all-gather.2.cloned.1.call-update) | async-done | bytes 2097168 | tf_op jit(solution)/shard_map/all_gather | solution.py:78
  273.0 7.5 %fusion.7 = f32[1024,256]{1,0:T(8,128)} fusion(bf16[4096,256]{1,0:T(8,128)(2,1)} %all-gather.2.cloned.1.call-done, bf16[4096,512]{1,0:T(8,128)(2,1)} %bitcast.41, bf16[4096,512]{1,0:T(8,128)(2,1)} %param.11), kind=kOutput, calls=%fused_computation.10 | convolution fusion | flops 2164260864 | bytes 11534336 | tf_op jit(solution)/shard_map/dot_general | solution.py:80
  281.1 74.1 %all-reduce.2 = (bf16[1024,256]{1,0:T(8,128)(2,1)}, f32[256]{0:T(256)}) all-reduce(f32[1024,256]{1,0:T(8,128)} %fusion.7, f32[256]{0:T(256)S(1)} %convert_reduce_fusion), channel_id=1, replica_groups=mesh['dom'=16,'feat'=2] {'dom'}, use_global_device_ids=true, to_apply=%region_1.2 | all-reduce | flops 262400 | bytes 1574912 | tf_op jit(solution)/shard_map/psum | solution.py:85
  (87 shorter events, 38.8 us)
Async XLA Ops:
  7.2 110.1 %copy-start = (bf16[1,102,128,128]{3,2,1,0:T(8,128)(2,1)S(1)}, bf16[1,102,128,128]{3,2,1,0:T(8,128)(2,1)}, u32[]{:S(2)}) copy-start(bf16[1,102,128,128]{3,2,1,0:T(8,128)(2,1)} %param.15) | copy-start | bytes 10027012
  7.2 18.7 %copy-start.13 = (s32[1,102]{1,0:T(1,128)S(1)}, s32[1,102]{1,0:T(1,128)}, u32[]{:S(2)}) copy-start(s32[1,102]{1,0:T(1,128)} %param.17) | copy-start | bytes 1228
  16.7 9.9 %collective-permute-start = (bf16[256,512]{1,0:T(8,128)(2,1)}, bf16[256,512]{1,0:T(8,128)(2,1)}, u32[]{:S(2)}, u32[]{:S(2)}) collective-permute-start(bf16[256,512]{1,0:T(8,128)(2,1)} %get-tuple-element.7), channel_id=1, source_target_pairs={{0,2},{2,4},{4,6},{6,8},{8,10},{10,12},{12,14},{14,16},{16,18},{18... | collective-permute-start | bytes 786440 | tf_op jit(solution)/shard_map/ppermute | solution.py:17
  17.2 10.4 %collective-permute-start.1 = (bf16[256,512]{1,0:T(8,128)(2,1)}, bf16[256,512]{1,0:T(8,128)(2,1)}, u32[]{:S(2)}, u32[]{:S(2)}) collective-permute-start(bf16[256,512]{1,0:T(8,128)(2,1)} %get-tuple-element.7), channel_id=1, source_target_pairs={{0,30},{2,0},{4,2},{6,4},{8,6},{10,8},{12,10},{14,12},{16,14},{18,... | collective-permute-start | bytes 786440 | tf_op jit(solution)/shard_map/ppermute | solution.py:20
  22.1 13.4 %all-to-all-start = ((s32[1,16,128]{2,0,1:T(1,128)}), s32[1,16,128]{2,0,1:T(1,128)S(1)}, u32[]{:S(2)}, u32[]{:S(2)}) async-start(s32[1,16,128]{2,0,1:T(1,128)} %bitcast.4), calls=%async_computation | async-start | bytes 16384 | tf_op jit(solution)/shard_map/all_to_all | solution.py:58
  25.8 210.9 %reduce-scatter.2.cloned.1.call-start = ((), (), s32[]{:S(2)}) async-start(), calls=%async_computation.2 | async-start | bytes 6291456 | tf_op jit(solution)/shard_map/reduce_scatter | solution.py:69
  26.6 8.9 %collective-permute-start.2 = (bf16[256,512]{1,0:T(8,128)(2,1)}, bf16[256,512]{1,0:T(8,128)(2,1)}, u32[]{:S(2)}, u32[]{:S(2)}) collective-permute-start(bf16[256,512]{1,0:T(8,128)(2,1)} %collective-permute-done), channel_id=1, source_target_pairs={{0,2},{2,4},{4,6},{6,8},{8,10},{10,12},{12,14},{14,16},{16,18},{18... | collective-permute-start | bytes 786440 | tf_op jit(solution)/shard_map/ppermute | solution.py:17
  27.6 8.7 %collective-permute-start.3 = (bf16[256,512]{1,0:T(8,128)(2,1)}, bf16[256,512]{1,0:T(8,128)(2,1)}, u32[]{:S(2)}, u32[]{:S(2)}) collective-permute-start(bf16[256,512]{1,0:T(8,128)(2,1)} %collective-permute-done.1), channel_id=1, source_target_pairs={{0,30},{2,0},{4,2},{6,4},{8,6},{10,8},{12,10},{14,12},{16,14},{18,... | collective-permute-start | bytes 786440 | tf_op jit(solution)/shard_map/ppermute | solution.py:20
  35.5 8.9 %collective-permute-start.4 = (bf16[256,512]{1,0:T(8,128)(2,1)}, bf16[256,512]{1,0:T(8,128)(2,1)}, u32[]{:S(2)}, u32[]{:S(2)}) collective-permute-start(bf16[256,512]{1,0:T(8,128)(2,1)} %collective-permute-done.2), channel_id=1, source_target_pairs={{0,2},{2,4},{4,6},{6,8},{8,10},{10,12},{12,14},{14,16},{16,18},{18... | collective-permute-start | bytes 786440 | tf_op jit(solution)/shard_map/ppermute | solution.py:17
  36.3 9.9 %collective-permute-start.5 = (bf16[256,512]{1,0:T(8,128)(2,1)}, bf16[256,512]{1,0:T(8,128)(2,1)S(1)}, u32[]{:S(2)}, u32[]{:S(2)}) collective-permute-start(bf16[256,512]{1,0:T(8,128)(2,1)} %collective-permute-done.3), channel_id=1, source_target_pairs={{0,30},{2,0},{4,2},{6,4},{8,6},{10,8},{12,10},{14,12},{16,14},{18,... | collective-permute-start | bytes 786440 | tf_op jit(solution)/shard_map/ppermute | solution.py:20
  44.4 8.8 %collective-permute-start.6 = (bf16[256,512]{1,0:T(8,128)(2,1)}, bf16[256,512]{1,0:T(8,128)(2,1)S(1)}, u32[]{:S(2)}, u32[]{:S(2)}) collective-permute-start(bf16[256,512]{1,0:T(8,128)(2,1)} %collective-permute-done.4), channel_id=1, source_target_pairs={{0,2},{2,4},{4,6},{6,8},{8,10},{10,12},{12,14},{14,16},{16,18},{18... | collective-permute-start | bytes 786440 | tf_op jit(solution)/shard_map/ppermute | solution.py:17
  46.2 10.4 %collective-permute-start.7 = (bf16[256,512]{1,0:T(8,128)(2,1)S(1)}, bf16[256,512]{1,0:T(8,128)(2,1)S(1)}, u32[]{:S(2)}, u32[]{:S(2)}) collective-permute-start(bf16[256,512]{1,0:T(8,128)(2,1)S(1)} %collective-permute-done.5), channel_id=1, source_target_pairs={{0,30},{2,0},{4,2},{6,4},{8,6},{10,8},{12,10},{14,12},{16,14},{18,... | collective-permute-start | bytes 786440 | tf_op jit(solution)/shard_map/ppermute | solution.py:20
  53.2 9.5 %collective-permute-start.8 = (bf16[256,512]{1,0:T(8,128)(2,1)S(1)}, bf16[256,512]{1,0:T(8,128)(2,1)S(1)}, u32[]{:S(2)}, u32[]{:S(2)}) collective-permute-start(bf16[256,512]{1,0:T(8,128)(2,1)S(1)} %collective-permute-done.6), channel_id=1, source_target_pairs={{0,2},{2,4},{4,6},{6,8},{8,10},{10,12},{12,14},{14,16},{16,18},{18... | collective-permute-start | bytes 786440 | tf_op jit(solution)/shard_map/ppermute | solution.py:17
  56.6 8.3 %collective-permute-start.9 = (bf16[256,512]{1,0:T(8,128)(2,1)S(1)}, bf16[256,512]{1,0:T(8,128)(2,1)S(1)}, u32[]{:S(2)}, u32[]{:S(2)}) collective-permute-start(bf16[256,512]{1,0:T(8,128)(2,1)S(1)} %collective-permute-done.7), channel_id=1, source_target_pairs={{0,30},{2,0},{4,2},{6,4},{8,6},{10,8},{12,10},{14,12},{16,14},{18,... | collective-permute-start | bytes 786440 | tf_op jit(solution)/shard_map/ppermute | solution.py:20
  62.7 8.6 %collective-permute-start.10 = (bf16[256,512]{1,0:T(8,128)(2,1)S(1)}, bf16[256,512]{1,0:T(8,128)(2,1)S(1)}, u32[]{:S(2)}, u32[]{:S(2)}) collective-permute-start(bf16[256,512]{1,0:T(8,128)(2,1)S(1)} %collective-permute-done.8), channel_id=1, source_target_pairs={{0,2},{2,4},{4,6},{6,8},{8,10},{10,12},{12,14},{14,16},{16,18},{18... | collective-permute-start | bytes 786440 | tf_op jit(solution)/shard_map/ppermute | solution.py:17
  64.9 8.6 %collective-permute-start.11 = (bf16[256,512]{1,0:T(8,128)(2,1)S(1)}, bf16[256,512]{1,0:T(8,128)(2,1)S(1)}, u32[]{:S(2)}, u32[]{:S(2)}) collective-permute-start(bf16[256,512]{1,0:T(8,128)(2,1)S(1)} %collective-permute-done.9), channel_id=1, source_target_pairs={{0,30},{2,0},{4,2},{6,4},{8,6},{10,8},{12,10},{14,12},{16,14},{18,... | collective-permute-start | bytes 786440 | tf_op jit(solution)/shard_map/ppermute | solution.py:20
  71.3 8.6 %collective-permute-start.12 = (bf16[256,512]{1,0:T(8,128)(2,1)S(1)}, bf16[256,512]{1,0:T(8,128)(2,1)S(1)}, u32[]{:S(2)}, u32[]{:S(2)}) collective-permute-start(bf16[256,512]{1,0:T(8,128)(2,1)S(1)} %collective-permute-done.10), channel_id=1, source_target_pairs={{0,2},{2,4},{4,6},{6,8},{8,10},{10,12},{12,14},{14,16},{16,18},{18... | collective-permute-start | bytes 786440 | tf_op jit(solution)/shard_map/ppermute | solution.py:17
  73.5 8.6 %collective-permute-start.13 = (bf16[256,512]{1,0:T(8,128)(2,1)S(1)}, bf16[256,512]{1,0:T(8,128)(2,1)S(1)}, u32[]{:S(2)}, u32[]{:S(2)}) collective-permute-start(bf16[256,512]{1,0:T(8,128)(2,1)S(1)} %collective-permute-done.11), channel_id=1, source_target_pairs={{0,30},{2,0},{4,2},{6,4},{8,6},{10,8},{12,10},{14,12},{16,14},{18,... | collective-permute-start | bytes 786440 | tf_op jit(solution)/shard_map/ppermute | solution.py:20
  79.9 8.5 %collective-permute-start.14 = (bf16[256,512]{1,0:T(8,128)(2,1)S(1)}, bf16[256,512]{1,0:T(8,128)(2,1)S(1)}, u32[]{:S(2)}, u32[]{:S(2)}) collective-permute-start(bf16[256,512]{1,0:T(8,128)(2,1)S(1)} %collective-permute-done.12), channel_id=1, source_target_pairs={{0,2},{2,4},{4,6},{6,8},{8,10},{10,12},{12,14},{14,16},{16,18},{18... | collective-permute-start | bytes 786440 | tf_op jit(solution)/shard_map/ppermute | solution.py:17
  131.1 28.4 %copy-start.10 = (s32[1,102]{1,0:T(1,128)S(1)}, s32[1,102]{1,0:T(1,128)}, u32[]{:S(2)}) copy-start(s32[1,102]{1,0:T(1,128)} %param.16) | copy-start | bytes 1228
  184.4 52.3 %copy-start.7 = (bf16[2048,256]{1,0:T(8,128)(2,1)S(1)}, bf16[2048,256]{1,0:T(8,128)(2,1)}, u32[]{:S(2)}) copy-start(bf16[2048,256]{1,0:T(8,128)(2,1)} %param.21) | copy-start | bytes 3145732
  184.4 52.3 %copy-start.9 = (f32[256]{0:T(256)S(1)}, f32[256]{0:T(256)}, u32[]{:S(2)}) copy-start(f32[256]{0:T(256)} %param.14) | copy-start | bytes 3076
  184.4 88.6 %all-gather.2.cloned.1.call-start = ((), (), s32[]{:S(2)}) async-start(), calls=%async_computation.3 | async-start | bytes 3145728 | tf_op jit(solution)/shard_map/all_gather | solution.py:78
  273.0 84.1 %copy-start.1 = (bf16[1,102,128,128]{3,2,1,0:T(8,128)(2,1)S(1)}, bf16[1,102,128,128]{3,2,1,0:T(8,128)(2,1)}, u32[]{:S(2)}) copy-start(bf16[1,102,128,128]{3,2,1,0:T(8,128)(2,1)} %param.15) | copy-start | bytes 10027012
  (8 other events, 30.8 us)
Sparse Core Ops, SparseCore 0:
  184.5 52.1 reduce-scatter.1
  239.9 33.0 all-gather.1
